TPU v7x, 32 devices: a whole 2x2x4 slice. The times are simulated.
32 devices in a mesh: seq: 8 (over z, core), fsdp: 4 (over y, x).
Axes of the slice: x: 2, y: 2, z: 4, core: 2. Of those that a mesh axis runs over, the one named last changes fastest.
Arguments:
- signal: bfloat16 [4, 8192, 1024], P('fsdp', 'seq'), may hold values from -6 to 6
- cotangent: bfloat16 [4, 8192, 1024], P('fsdp', 'seq'), may hold values from -6 to 6
- w_in: bfloat16 [1024, 1024], P('fsdp'), may hold values from -0.1875 to 0.1875
- w_conv: bfloat16 [2, 1024, 128], P(None, 'seq'), may hold values from -0.5 to 0.5
- w_out: bfloat16 [1024, 1024], P('fsdp'), may hold values from -0.1875 to 0.1875
- dilation: int32 [16], P('seq'), may hold values from 512 to 4095
- lengths: int32 [4], P('fsdp'), may hold values from 2048 to 8192, as said below
Outputs:
- grad_signal: bfloat16 [4, 8192, 1024], P('fsdp', 'seq')
- grad_in: float32 [1024, 1024], P('fsdp')
- grad_out: float32 [1024, 1024], P('fsdp')
- grad_conv: float32 [2, 1024, 128], P(None, 'seq')
Inputs may be any that keep to these rules, and one draw needn't show every extreme that they name: `lengths`: some record in every draw holds all 8192 samples.
All inputs are finite; a program needn't handle non-finite values.
Results may differ from a plain program's by a relative error of at most 0.0068.
Values may be sent and summed in bfloat16 or wider, within the bound.
No kernel may reach another device: no remote copies, remote signals or barrier semaphores. Data moves between devices by JAX's collectives and lax.ppermute only.
A program may use at most 128 MiB of HBM per device.

v0:
```python
import math
import jax
import jax.numpy as jnp
from jax import lax
from jax.sharding import PartitionSpec as P


def delayed(series, amount):
    padded = jnp.concatenate([jnp.zeros_like(series), series], axis=0)
    return lax.dynamic_slice_in_dim(padded, series.shape[0] - amount, series.shape[0], 0)


def advanced(series, amount):
    padded = jnp.concatenate([series, jnp.zeros_like(series)], axis=0)
    return lax.dynamic_slice_in_dim(padded, amount, series.shape[0], 0)


def group_pass(projected, grad_gated, kernel, amount, live_mask):
    group_width = kernel.shape[0] // 2
    stacked = jnp.concatenate([projected, delayed(projected, amount)], axis=1)
    pre_acts = jnp.dot(stacked, kernel, preferred_element_type=jnp.float32)
    tanh_act = jnp.tanh(pre_acts[:, :group_width])
    sig_act = jax.nn.sigmoid(pre_acts[:, group_width:])
    masked = live_mask[:, None]
    gated_out = (tanh_act * sig_act * masked).astype(jnp.bfloat16)
    grad_masked = grad_gated.astype(jnp.float32) * masked
    grad_filter = grad_masked * sig_act * (1.0 - tanh_act * tanh_act)
    grad_gate = grad_masked * tanh_act * sig_act * (1.0 - sig_act)
    grad_acts = jnp.concatenate([grad_filter, grad_gate], axis=1).astype(jnp.bfloat16)
    grad_kernel = jnp.dot(stacked.T, grad_acts, preferred_element_type=jnp.float32)
    paired = jnp.concatenate([grad_acts, advanced(grad_acts, amount)], axis=1)
    back_kernel = jnp.concatenate([kernel[:group_width].T, kernel[group_width:].T], axis=0)
    grad_mixed = jnp.dot(paired, back_kernel, preferred_element_type=jnp.float32).astype(
        jnp.bfloat16
    )
    return (gated_out, grad_mixed, grad_kernel)


def column_order(series, fsdp_size, seq_size):
    samples, channels = series.shape
    quarter = channels // (fsdp_size * seq_size)
    return (
        series.reshape(samples, fsdp_size, seq_size, quarter)
        .transpose(0, 2, 1, 3)
        .reshape(samples, channels)
    )


def outer_terms(left_side, right_side):
    return lax.dot_general(
        left_side, right_side, (((0,), (0,)), ((), ())), preferred_element_type=jnp.float32
    )


def local(signal, cotangent, w_in, w_conv, w_out, dilation, lengths):
    record = signal[0]
    upstream = cotangent[0]
    samples, channels = record.shape
    seq_size = lax.axis_size("seq")
    fsdp_size = lax.axis_size("fsdp")
    full_len = samples * seq_size
    local_groups = dilation.shape[0]
    local_chans = w_conv.shape[1]
    group_width = local_chans // local_groups
    factor = 1.0 / math.sqrt(full_len * fsdp_size)
    projected = jnp.dot(
        record, lax.all_gather(w_in, "fsdp", axis=0, tiled=True), preferred_element_type=jnp.float32
    ).astype(jnp.bfloat16)
    grad_gated = lax.dot_general(
        upstream,
        lax.all_gather(w_out, "fsdp", axis=0, tiled=True),
        (((1,), (1,)), ((), ())),
        preferred_element_type=jnp.float32,
    ).astype(jnp.bfloat16)
    proj_groups, grad_groups = (
        lax.all_to_all(projected, "seq", split_axis=1, concat_axis=0, tiled=True),
        lax.all_to_all(grad_gated, "seq", split_axis=1, concat_axis=0, tiled=True),
    )
    live_mask = (jnp.arange(full_len, dtype=jnp.int32) < lengths[0]).astype(jnp.float32)
    gated_parts = []
    mixed_parts = []
    tap_zero = []
    tap_one = []
    for group_index in range(local_groups):
        low_chan = group_index * group_width
        kernel = jnp.concatenate(
            [
                w_conv[0, low_chan : low_chan + group_width],
                w_conv[1, low_chan : low_chan + group_width],
            ],
            axis=0,
        )
        gated_out, grad_mixed, grad_kernel = group_pass(
            proj_groups[:, low_chan : low_chan + group_width],
            grad_groups[:, low_chan : low_chan + group_width],
            kernel,
            dilation[group_index],
            live_mask,
        )
        gated_parts.append(gated_out)
        mixed_parts.append(grad_mixed)
        tap_zero.append(grad_kernel[:group_width])
        tap_one.append(grad_kernel[group_width:])
    gated_groups = jnp.concatenate(gated_parts, axis=1)
    mixed_groups = jnp.concatenate(mixed_parts, axis=1)
    conv_local = jnp.stack(
        [jnp.concatenate(tap_zero, axis=0), jnp.concatenate(tap_one, axis=0)], axis=0
    )
    conv_total = lax.psum(conv_local, "fsdp")
    gated_time, mixed_time = (
        lax.all_to_all(gated_groups, "seq", split_axis=0, concat_axis=1, tiled=True),
        lax.all_to_all(mixed_groups, "seq", split_axis=0, concat_axis=1, tiled=True),
    )
    mixed_back = lax.dot_general(
        mixed_time,
        lax.all_gather(w_in, "fsdp", axis=0, tiled=True),
        (((1,), (1,)), ((), ())),
        preferred_element_type=jnp.float32,
    )
    grad_signal = (upstream.astype(jnp.float32) + mixed_back).astype(jnp.bfloat16)[None]
    gated_order = column_order(gated_time, fsdp_size, seq_size)
    record_order = column_order(record, fsdp_size, seq_size)
    part_out = lax.psum_scatter(
        outer_terms(gated_order, upstream), ("seq", "fsdp"), scatter_dimension=0, tiled=True
    )
    part_in = lax.psum_scatter(
        outer_terms(record_order, mixed_time), ("seq", "fsdp"), scatter_dimension=0, tiled=True
    )
    grad_in, grad_out = (
        lax.all_gather(part_in, "seq", axis=0, tiled=True),
        lax.all_gather(part_out, "seq", axis=0, tiled=True),
    )
    return (grad_signal, grad_in * factor, grad_out * factor, conv_total * factor)


def solution(mesh):
    placed = (
        P("fsdp", "seq", None),
        P("fsdp", "seq", None),
        P("fsdp", None),
        P(None, "seq", None),
        P("fsdp", None),
        P("seq"),
        P("fsdp"),
    )
    return jax.shard_map(
        local,
        mesh=mesh,
        in_specs=placed,
        out_specs=(P("fsdp", "seq", None), P("fsdp", None), P("fsdp", None), P(None, "seq", None)),
        check_vma=False,
    )
```

profile of v0, /device:TPU:0, one launch (start us, length us, event | category | flops | bytes accessed | tf_op | source)
XLA Modules:
  0.0 627.7 jit_solution(6793822717476289242)
XLA Ops:
  7.2 0.0 all-gather.7.cloned.1.call-start
  7.2 0.7 all-gather.7.cloned.1.call-update
  7.9 0.0 all-gather.5.cloned.1.call-start
  7.9 0.7 all-gather.5.cloned.1.call-update
  8.6 39.1 %all-gather.7.cloned.1.call-done = bf16[1024,1024]{1,0:T(8,128)(2,1)} async-done(((bf16[256,1024]{1,0:T(8,128)(2,1)}), bf16[1024,1024]{1,0:T(8,128)(2,1)}) %all-gather.7.cloned.1.call-update) | async-done | bytes 2097168 | tf_op jit(solution)/shard_map/all_gather | solution.py:67
  47.8 4.6 fusion.26
  52.4 2.4 copy.26
  54.7 4.6 all-to-all-start.1
  59.3 25.5 %all-gather.5.cloned.1.call-done = bf16[1024,1024]{1,0:T(8,128)(2,1)} async-done(((bf16[256,1024]{1,0:T(8,128)(2,1)}), bf16[1024,1024]{1,0:T(8,128)(2,1)}) %all-gather.5.cloned.1.call-update) | async-done | bytes 2097168 | tf_op jit(solution)/shard_map/all_gather | solution.py:71
  84.8 6.0 fusion.23
  90.8 17.6 %all-to-all-done.1 = bf16[1024,8,128]{2,0,1:T(8,128)(2,1)S(1)} async-done(((bf16[1024,8,128]{2,0,1:T(8,128)(2,1)}), bf16[1024,8,128]{2,0,1:T(8,128)(2,1)S(1)}, u32[]{:S(2)}, u32[]{:S(2)}) %all-to-all-start.1) | async-done | bytes 2097184 | tf_op jit(solution)/shard_map/all_to_all | solution.py:76
  108.4 4.7 all-to-all-start
  113.1 0.6 fusion.55
  116.7 2.7 fusion.52
  119.4 42.5 %all-to-all-done = bf16[1024,8,128]{0,2,1:T(8,128)(2,1)} async-done(((bf16[1024,8,128]{0,2,1:T(8,128)(2,1)}), bf16[1024,8,128]{0,2,1:T(8,128)(2,1)}, u32[]{:S(2)}, u32[]{:S(2)}) %all-to-all-start) | async-done | bytes 2097184 | tf_op jit(solution)/shard_map/all_to_all | solution.py:77
  161.9 1.9 copy.42
  163.9 0.3 copy-done
  164.1 0.6 copy-done.1
  164.8 8.6 %pad_dynamic-slice_fusion.1 = (bf16[8192,64]{1,0:T(8,128)(2,1)S(1)}, bf16[8192,64]{1,0:T(8,128)(2,1)S(1)}) fusion(s32[]{:T(128)S(6)} %select_n.14, bf16[8192,64]{1,0:T(8,128)(2,1)S(1)} %copy-done, s32[]{:T(128)S(6)} %select_n.12, bf16[8192,64]{1,0:T(8,128)(2,1)S(1)} %copy-done.1), kind=kLoop, calls=%fused_computation.14 | loop fusion | bytes 4194312 | tf_op jit(solution)/shard_map/dynamic_slice | solution.py:10
  173.4 1.3 fusion.32
  174.7 0.1 copy-done.4
  174.8 0.6 copy-done.2
  175.4 1.5 fusion.30
  176.9 3.7 multiply_convert_fusion.3
  180.6 0.2 pad_maximum_fusion.5
  180.8 1.5 copy.45
  182.3 4.3 all-to-all-start.3
  186.7 0.0 reduce-scatter.9.cloned.1.call-start
  190.3 3.1 pad_maximum_fusion.1
  193.4 42.3 %all-to-all-done.3 = bf16[8,1024,128]{1,2,0:T(8,128)(2,1)} async-done(((bf16[8,1024,128]{1,2,0:T(8,128)(2,1)}), bf16[8,1024,128]{1,2,0:T(8,128)(2,1)}, u32[]{:S(2)}, u32[]{:S(2)}) %all-to-all-start.3) | async-done | bytes 2097184 | tf_op jit(solution)/shard_map/all_to_all | solution.py:111
  235.7 1.9 copy.32
  237.6 0.3 copy-done.11
  237.9 4.3 fusion.19
  242.2 0.0 reduce-scatter.9.cloned.1.call-update
  242.3 2.4 pad_dynamic-slice_fusion.2
  244.8 1.0 convolution_convert_fusion.1
  245.8 0.2 copy-done.5
  246.0 0.2 pad_maximum_fusion.3
  246.2 0.8 pad_dynamic-slice_fusion
  246.9 1.0 convolution_convert_fusion
  248.0 0.2 pad_maximum_fusion.4
  248.2 1.6 copy.46
  249.8 4.4 all-to-all-start.2
  254.1 0.0 reduce-scatter.7.cloned.1.call-start
  254.2 4.0 copy.28
  258.2 3.3 copy.29
  261.4 49.1 %all-to-all-done.2 = bf16[8,1024,128]{1,2,0:T(8,128)(2,1)} async-done(((bf16[8,1024,128]{1,2,0:T(8,128)(2,1)}), bf16[8,1024,128]{1,2,0:T(8,128)(2,1)}, u32[]{:S(2)}, u32[]{:S(2)}) %all-to-all-start.2) | async-done | bytes 2097184 | tf_op jit(solution)/shard_map/all_to_all | solution.py:112
  310.5 6.6 %convolution_bitcast_fusion = f32[1024,1024]{0,1:T(8,128)} fusion(bf16[1024,1024]{0,1:T(8,128)(2,1)} %bitcast.20, bf16[1024,1024]{0,1:T(8,128)(2,1)} %bitcast.91), kind=kOutput, calls=%fused_computation.17 | convolution fusion | flops 2147483648 | bytes 8388608 | tf_op jit(solution)/shard_map/dot_general | solution.py:50
  317.1 5.5 copy.36
  322.7 0.3 all-reduce.6.cloned.1.call-start
  323.0 4.5 fusion.31
  327.5 1.6 fusion.29
  329.2 0.7 pad_maximum_fusion.10
  329.9 0.0 all-gather.11.cloned.1.call-start
  329.9 56.5 %reduce-scatter.9.cloned.1.call-done = f32[32,1024]{1,0:T(8,128)} async-done(((f32[1024,1024]{1,0:T(8,128)}), f32[32,1024]{1,0:T(8,128)}) %reduce-scatter.9.cloned.1.call-update) | async-done | bytes 131088 | tf_op jit(solution)/shard_map/reduce_scatter | solution.py:123
  386.5 0.0 all-gather.9.cloned.1.call-start
  386.5 142.3 %reduce-scatter.7.cloned.1.call-done = f32[32,1024]{1,0:T(8,128)} async-done(((f32[1024,1024]{1,0:T(8,128)}), f32[32,1024]{1,0:T(8,128)}) %reduce-scatter.7.cloned.1.call-update) | async-done | bytes 131088 | tf_op jit(solution)/shard_map/reduce_scatter | solution.py:126
  528.8 42.5 %all-reduce.6.cloned.1.call-done = f32[2,128,128]{2,1,0:T(8,128)} async-done(((f32[2,128,128]{2,1,0:T(8,128)}), f32[2,128,128]{2,1,0:T(8,128)}) %all-reduce.6.cloned.1.call-update) | async-done | bytes 131088 | tf_op jit(solution)/shard_map/psum | solution.py:109
  571.3 1.6 broadcast_multiply_fusion.2
  572.9 6.6 %fusion.10 = bf16[1,1024,1024]{2,1,0:T(8,128)(2,1)} fusion(bf16[1,1024,1024]{2,1,0:T(8,128)(2,1)} %param.8, bf16[1024,1024]{0,1:T(8,128)(2,1)} %bitcast.20, bf16[1024,1024]{1,0:T(8,128)(2,1)} %all-gather.7.cloned.1.call-done), kind=kOutput, calls=%fused_computation.18 | convolution fusion | flops 2150629376 | bytes 8388608 | tf_op jit(solution)/shard_map/dot_general | solution.py:114
  579.5 15.6 %all-gather.11.cloned.1.call-done = f32[256,1024]{1,0:T(8,128)} async-done(((f32[32,1024]{1,0:T(8,128)}), f32[256,1024]{1,0:T(8,128)}) %all-gather.11.cloned.1.call-update) | async-done | bytes 1048592 | tf_op jit(solution)/shard_map/all_gather | solution.py:131
  595.1 2.3 broadcast_multiply_fusion
  597.4 21.1 %all-gather.9.cloned.1.call-done = f32[256,1024]{1,0:T(8,128)} async-done(((f32[32,1024]{1,0:T(8,128)}), f32[256,1024]{1,0:T(8,128)}) %all-gather.9.cloned.1.call-update) | async-done | bytes 1048592 | tf_op jit(solution)/shard_map/all_gather | solution.py:130
  618.5 2.3 broadcast_multiply_fusion.1
  (28 shorter events, 0.2 us)
Async XLA Ops:
  7.2 40.6 %all-gather.7.cloned.1.call-start = ((), (), s32[]{:S(2)}) async-start(), calls=%async_computation.7 | async-start | bytes 2621440 | tf_op jit(solution)/shard_map/all_gather | solution.py:67
  7.9 76.9 %all-gather.5.cloned.1.call-start = ((), (), s32[]{:S(2)}) async-start(), calls=%async_computation.6 | async-start | bytes 2621440 | tf_op jit(solution)/shard_map/all_gather | solution.py:71
  54.7 53.6 %all-to-all-start.1 = ((bf16[1024,8,128]{2,0,1:T(8,128)(2,1)}), bf16[1024,8,128]{2,0,1:T(8,128)(2,1)S(1)}, u32[]{:S(2)}, u32[]{:S(2)}) async-start(bf16[1024,8,128]{2,0,1:T(8,128)(2,1)} %copy.26), calls=%async_computation.1 | async-start | bytes 4194304 | tf_op jit(solution)/shard_map/all_to_all | solution.py:76
  108.4 4.7 copy-start.10
  108.4 8.3 %copy-start.9 = (bf16[2,128,128]{2,1,0:T(8,128)(2,1)S(1)}, bf16[2,128,128]{2,1,0:T(8,128)(2,1)}, u32[]{:S(2)}) copy-start(bf16[2,128,128]{2,1,0:T(8,128)(2,1)} %param.10) | copy-start | bytes 196612
  108.4 53.5 %all-to-all-start = ((bf16[1024,8,128]{0,2,1:T(8,128)(2,1)}), bf16[1024,8,128]{0,2,1:T(8,128)(2,1)}, u32[]{:S(2)}, u32[]{:S(2)}) async-start(bf16[1024,8,128]{0,2,1:T(8,128)(2,1)} %bitcast.90), calls=%async_computation | async-start | bytes 4194304 | tf_op jit(solution)/shard_map/all_to_all | solution.py:77
  161.9 2.2 copy-start
  161.9 2.9 copy-start.1
  173.4 1.4 copy-start.4
  173.4 2.0 copy-start.2
  182.3 53.4 %all-to-all-start.3 = ((bf16[8,1024,128]{1,2,0:T(8,128)(2,1)}), bf16[8,1024,128]{1,2,0:T(8,128)(2,1)}, u32[]{:S(2)}, u32[]{:S(2)}) async-start(bf16[8,1024,128]{1,2,0:T(8,128)(2,1)} %bitcast.84), calls=%async_computation.3 | async-start | bytes 4194304 | tf_op jit(solution)/shard_map/all_to_all | solution.py:111
  186.7 199.8 %reduce-scatter.9.cloned.1.call-start = ((), (), s32[]{:S(2)}) async-start(), calls=%async_computation.12 | async-start | bytes 4325376 | tf_op jit(solution)/shard_map/reduce_scatter | solution.py:123
  235.7 2.2 copy-start.11
  242.3 2.5 copy-start.7
  242.3 2.5 copy-start.8
  244.7 1.2 copy-start.5
  249.8 60.8 %all-to-all-start.2 = ((bf16[8,1024,128]{1,2,0:T(8,128)(2,1)}), bf16[8,1024,128]{1,2,0:T(8,128)(2,1)}, u32[]{:S(2)}, u32[]{:S(2)}) async-start(bf16[8,1024,128]{1,2,0:T(8,128)(2,1)} %bitcast.85), calls=%async_computation.2 | async-start | bytes 4194304 | tf_op jit(solution)/shard_map/all_to_all | solution.py:112
  254.1 274.7 %reduce-scatter.7.cloned.1.call-start = ((), (), s32[]{:S(2)}) async-start(), calls=%async_computation.11 | async-start | bytes 4325376 | tf_op jit(solution)/shard_map/reduce_scatter | solution.py:126
  322.7 248.7 %all-reduce.6.cloned.1.call-start = ((), (), s32[]{:S(2)}) async-start(), calls=%async_computation.10 | async-start | bytes 262144 | tf_op jit(solution)/shard_map/psum | solution.py:109
  323.0 4.5 copy-start.3
  323.0 4.5 copy-start.6
  329.9 265.2 %all-gather.11.cloned.1.call-start = ((), (), s32[]{:S(2)}) async-start(), calls=%async_computation.9 | async-start | bytes 1179648 | tf_op jit(solution)/shard_map/all_gather | solution.py:131
  386.5 232.0 %all-gather.9.cloned.1.call-start = ((), (), s32[]{:S(2)}) async-start(), calls=%async_computation.8 | async-start | bytes 1179648 | tf_op jit(solution)/shard_map/all_gather | solution.py:130
Sparse Core Ops, SparseCore 0:
  9.8 37.8 all-gather.6
  49.6 35.1 all-gather.4
  242.4 144.0 reduce-scatter.8
  388.6 140.1 reduce-scatter.6
  532.1 39.1 all-reduce.5
  572.8 22.2 all-gather.10
  596.7 21.8 all-gather.8
where the time goes:
time: 629 us; the launch traced here: 628 us
  waiting for transfers between devices  496 us (79%)
  local copies, waits for them, and re-layouts  39.4 us (6%)
  matrix products  38.9 us (6%)
  between operations  21 us (3%)
  starting transfers between devices  18.5 us (3%)
  other arithmetic  14.3 us (2%)
    reduce_scatter x1, waiting for transfers between devices, local(): lax.psum_scatter(outer_terms(record_order, mixed_time), ('seq', 'fsdp'),...  142 us
    reduce_scatter x1, waiting for transfers between devices, local(): lax.psum_scatter(outer_terms(gated_order, upstream), ('seq', 'fsdp'), sca...  56.5 us
    all_to_all x1, waiting for transfers between devices, local(): lax.all_to_all(mixed_groups, 'seq', split_axis=0, concat_axis=1, tiled=True)  49.1 us
    psum x1, waiting for transfers between devices, local(): conv_total = lax.psum(conv_local, 'fsdp')  42.5 us
    all_to_all x1, waiting for transfers between devices, local(): lax.all_to_all(grad_gated, 'seq', split_axis=1, concat_axis=0, tiled=True)  42.5 us
    all_to_all x1, waiting for transfers between devices, local(): lax.all_to_all(gated_groups, 'seq', split_axis=0, concat_axis=1, tiled=True)  42.3 us
    all_gather x1, waiting for transfers between devices, local(): lax.all_gather(w_in, 'fsdp', axis=0, tiled=True)  39.1 us
    all_gather x1, waiting for transfers between devices, local(): lax.all_gather(w_out, 'fsdp', axis=0, tiled=True)  25.5 us
  transfers between devices with their start and end apart: 11, of which 11 were waited for; matrix products, arithmetic and copies ran while one was open for 10% of the time, Pallas kernels for 0%

commit v1 on v0

--- a/solution.py
+++ b/solution.py
@@ -1,8 +1,29 @@
+import functools
 import math
 import jax
 import jax.numpy as jnp
 from jax import lax
 from jax.sharding import PartitionSpec as P
+from jax.lax import ppermute, psum
+
+
+def replace_pieces_all(own_rows, row_axis):
+    fan = psum(1, axis_name=row_axis)
+
+    def match_the_zones(work_now, z_new):
+        if z_new >= fan:
+            return work_now
+        low = match_the_zones(
+            work_now + ppermute(work_now, row_axis, tuple(((i, i ^ z_new) for i in range(fan)))),
+            2 * z_new,
+        )
+        return low
+
+    upper = match_the_zones(own_rows, 1)
+    return upper
+
+
+scan_the_circles = functools.partial(replace_pieces_all, row_axis="fsdp")
 
 
 def delayed(series, amount):
@@ -106,7 +127,7 @@
     conv_local = jnp.stack(
         [jnp.concatenate(tap_zero, axis=0), jnp.concatenate(tap_one, axis=0)], axis=0
     )
-    conv_total = lax.psum(conv_local, "fsdp")
+    conv_total = scan_the_circles(conv_local)
     gated_time, mixed_time = (
         lax.all_to_all(gated_groups, "seq", split_axis=0, concat_axis=1, tiled=True),
         lax.all_to_all(mixed_groups, "seq", split_axis=0, concat_axis=1, tiled=True),

time: 629 us -> 582 us (0.925)
  waiting for transfers between devices: 496 us -> 451 us
    psum x1 -> x0, waiting for transfers between devices: 42.5 us -> none  [local(): conv_total = lax.psum(conv_local, 'fsdp')]
    all_gather x1, waiting for transfers between devices: 15.6 us -> 2.55 us  [local(): lax.all_gather(part_out, 'seq', axis=0, tiled=True)]
    ppermute x0 -> x2, waiting for transfers between devices: none -> 9.91 us  [match_the_zones(): ppermute(work_now, row_axis, tuple(((i, i ^ z_new) for i in range(fan))))]
    reduce_scatter x1, waiting for transfers between devices: 56.5 us -> 63.7 us  [local(): lax.psum_scatter(outer_terms(gated_order, upstream), ('seq', 'fsdp'), sca...]
  transfers between devices with their start and end apart: 11 -> 12, of which waited for: 11 -> 12; matrix products, arithmetic and copies ran while one was open for 10% -> 11% of each run, Pallas kernels for 0% -> 0%
where the time goes in v1:
time: 582 us; the launch traced here: 581 us
  waiting for transfers between devices  451 us (77%)
  local copies, waits for them, and re-layouts  39.4 us (7%)
  matrix products  38.9 us (7%)
  between operations  21.2 us (4%)
  starting transfers between devices  18.6 us (3%)
  other arithmetic  12.8 us (2%)
    reduce_scatter x1, waiting for transfers between devices, local(): lax.psum_scatter(outer_terms(record_order, mixed_time), ('seq', 'fsdp'),...  136 us
    reduce_scatter x1, waiting for transfers between devices, local(): lax.psum_scatter(outer_terms(gated_order, upstream), ('seq', 'fsdp'), sca...  63.7 us
    all_to_all x1, waiting for transfers between devices, local(): lax.all_to_all(mixed_groups, 'seq', split_axis=0, concat_axis=1, tiled=True)  49.1 us
    all_to_all x1, waiting for transfers between devices, local(): lax.all_to_all(grad_gated, 'seq', split_axis=1, concat_axis=0, tiled=True)  42.4 us
    all_to_all x1, waiting for transfers between devices, local(): lax.all_to_all(gated_groups, 'seq', split_axis=0, concat_axis=1, tiled=True)  42.2 us
    all_gather x1, waiting for transfers between devices, local(): lax.all_gather(w_in, 'fsdp', axis=0, tiled=True)  39.1 us
    all_gather x1, waiting for transfers between devices, local(): lax.all_gather(w_out, 'fsdp', axis=0, tiled=True)  25.5 us
    all_gather x1, waiting for transfers between devices, local(): lax.all_gather(part_in, 'seq', axis=0, tiled=True)  21 us
  transfers between devices with their start and end apart: 12, of which 12 were waited for; matrix products, arithmetic and copies ran while one was open for 11% of the time, Pallas kernels for 0%

profile of v1, /device:TPU:0, one launch (start us, length us, event | category | flops | bytes accessed | tf_op | source)
XLA Modules:
  0.0 581.5 jit_solution(4977603245735271958)
XLA Ops:
  7.2 0.0 all-gather.7.cloned.1.call-start
  7.2 0.7 all-gather.7.cloned.1.call-update
  7.9 0.0 all-gather.5.cloned.1.call-start
  7.9 0.7 all-gather.5.cloned.1.call-update
  8.6 39.1 %all-gather.7.cloned.1.call-done = bf16[1024,1024]{1,0:T(8,128)(2,1)} async-done(((bf16[256,1024]{1,0:T(8,128)(2,1)}), bf16[1024,1024]{1,0:T(8,128)(2,1)}) %all-gather.7.cloned.1.call-update) | async-done | bytes 2097168 | tf_op jit(solution)/shard_map/all_gather | solution.py:88
  47.8 4.6 fusion.26
  52.4 2.4 copy.26
  54.7 4.6 all-to-all-start.1
  59.3 25.5 %all-gather.5.cloned.1.call-done = bf16[1024,1024]{1,0:T(8,128)(2,1)} async-done(((bf16[256,1024]{1,0:T(8,128)(2,1)}), bf16[1024,1024]{1,0:T(8,128)(2,1)}) %all-gather.5.cloned.1.call-update) | async-done | bytes 2097168 | tf_op jit(solution)/shard_map/all_gather | solution.py:92
  84.8 5.9 %fusion.23 = bf16[1024,1024]{0,1:T(8,128)(2,1)} fusion(bf16[1024,1024]{1,0:T(8,128)(2,1)} %all-gather.5.cloned.1.call-done, bf16[1,1024,1024]{2,1,0:T(8,128)(2,1)} %param.8), kind=kOutput, calls=%fused_computation.51 | convolution fusion | flops 2148532224 | bytes 6291456 | tf_op jit(solution)/shard_map/dot_general | solution.py:90
  90.7 17.6 %all-to-all-done.1 = bf16[1024,8,128]{2,0,1:T(8,128)(2,1)S(1)} async-done(((bf16[1024,8,128]{2,0,1:T(8,128)(2,1)}), bf16[1024,8,128]{2,0,1:T(8,128)(2,1)S(1)}, u32[]{:S(2)}, u32[]{:S(2)}) %all-to-all-start.1) | async-done | bytes 2097184 | tf_op jit(solution)/shard_map/all_to_all | solution.py:97
  108.4 4.7 all-to-all-start
  113.1 0.6 fusion.56
  116.8 2.7 fusion.53
  119.5 42.4 %all-to-all-done = bf16[1024,8,128]{0,2,1:T(8,128)(2,1)} async-done(((bf16[1024,8,128]{0,2,1:T(8,128)(2,1)}), bf16[1024,8,128]{0,2,1:T(8,128)(2,1)}, u32[]{:S(2)}, u32[]{:S(2)}) %all-to-all-start) | async-done | bytes 2097184 | tf_op jit(solution)/shard_map/all_to_all | solution.py:98
  161.9 1.9 copy.42
  163.9 0.3 copy-done
  164.1 0.6 copy-done.1
  164.8 8.6 %pad_dynamic-slice_fusion.1 = (bf16[8192,64]{1,0:T(8,128)(2,1)S(1)}, bf16[8192,64]{1,0:T(8,128)(2,1)S(1)}) fusion(s32[]{:T(128)S(6)} %select_n.14, bf16[8192,64]{1,0:T(8,128)(2,1)S(1)} %copy-done, s32[]{:T(128)S(6)} %select_n.12, bf16[8192,64]{1,0:T(8,128)(2,1)S(1)} %copy-done.1), kind=kLoop, calls=%fused_computation.14 | loop fusion | bytes 4194312 | tf_op jit(solution)/shard_map/dynamic_slice | solution.py:31
  173.4 1.3 fusion.32
  174.7 0.1 copy-done.4
  174.8 0.6 copy-done.2
  175.4 1.5 fusion.30
  176.9 3.7 multiply_convert_fusion.3
  180.6 0.2 pad_maximum_fusion.5
  180.8 1.5 copy.45
  182.3 4.4 all-to-all-start.3
  186.7 0.0 reduce-scatter.9.cloned.1.call-start
  190.4 3.1 pad_maximum_fusion.1
  193.5 42.2 %all-to-all-done.3 = bf16[8,1024,128]{1,2,0:T(8,128)(2,1)} async-done(((bf16[8,1024,128]{1,2,0:T(8,128)(2,1)}), bf16[8,1024,128]{1,2,0:T(8,128)(2,1)}, u32[]{:S(2)}, u32[]{:S(2)}) %all-to-all-start.3) | async-done | bytes 2097184 | tf_op jit(solution)/shard_map/all_to_all | solution.py:132
  235.7 1.9 copy.32
  237.6 0.3 copy-done.11
  237.9 4.3 fusion.19
  242.3 2.4 pad_dynamic-slice_fusion.2
  244.8 1.0 convolution_convert_fusion.1
  245.8 0.2 copy-done.5
  246.0 0.2 pad_maximum_fusion.3
  246.2 0.8 pad_dynamic-slice_fusion
  247.0 1.0 convolution_convert_fusion
  248.0 0.2 pad_maximum_fusion.4
  248.2 1.6 copy.46
  249.8 4.3 all-to-all-start.2
  254.1 0.0 reduce-scatter.7.cloned.1.call-start
  254.2 4.0 copy.28
  258.1 3.3 copy.29
  261.4 49.1 %all-to-all-done.2 = bf16[8,1024,128]{1,2,0:T(8,128)(2,1)} async-done(((bf16[8,1024,128]{1,2,0:T(8,128)(2,1)}), bf16[8,1024,128]{1,2,0:T(8,128)(2,1)}, u32[]{:S(2)}, u32[]{:S(2)}) %all-to-all-start.2) | async-done | bytes 2097184 | tf_op jit(solution)/shard_map/all_to_all | solution.py:133
  310.5 6.6 %convolution_bitcast_fusion = f32[1024,1024]{0,1:T(8,128)} fusion(bf16[1024,1024]{0,1:T(8,128)(2,1)} %bitcast.20, bf16[1024,1024]{0,1:T(8,128)(2,1)} %bitcast.91), kind=kOutput, calls=%fused_computation.17 | convolution fusion | flops 2147483648 | bytes 8388608 | tf_op jit(solution)/shard_map/dot_general | solution.py:71
  317.2 5.5 copy.36
  322.7 0.0 all-gather.11.cloned.1.call-start
  322.7 63.7 %reduce-scatter.9.cloned.1.call-done = f32[32,1024]{1,0:T(8,128)} async-done(((f32[1024,1024]{1,0:T(8,128)}), f32[32,1024]{1,0:T(8,128)}) %reduce-scatter.9.cloned.1.call-update) | async-done | bytes 131088 | tf_op jit(solution)/shard_map/reduce_scatter | solution.py:144
  386.5 0.3 all-gather.9.cloned.1.call-start
  386.8 4.5 fusion.31
  391.3 1.6 fusion.29
  392.9 136.1 %reduce-scatter.7.cloned.1.call-done = f32[32,1024]{1,0:T(8,128)} async-done(((f32[1024,1024]{1,0:T(8,128)}), f32[32,1024]{1,0:T(8,128)}) %reduce-scatter.7.cloned.1.call-update) | async-done | bytes 131088 | tf_op jit(solution)/shard_map/reduce_scatter | solution.py:147
  529.0 0.1 collective-permute-start
  529.1 5.0 collective-permute-done
  534.1 0.1 collective-permute-start.1
  534.2 5.0 collective-permute-done.1
  539.1 0.7 add_multiply_fusion
  539.8 6.6 %fusion.10 = bf16[1,1024,1024]{2,1,0:T(8,128)(2,1)} fusion(bf16[1,1024,1024]{2,1,0:T(8,128)(2,1)} %param.8, bf16[1024,1024]{0,1:T(8,128)(2,1)} %bitcast.20, bf16[1024,1024]{1,0:T(8,128)(2,1)} %all-gather.7.cloned.1.call-done), kind=kOutput, calls=%fused_computation.18 | convolution fusion | flops 2150629376 | bytes 8388608 | tf_op jit(solution)/shard_map/dot_general | solution.py:135
  546.4 2.6 all-gather.11.cloned.1.call-done
  549.0 2.3 broadcast_multiply_fusion
  551.3 21.0 %all-gather.9.cloned.1.call-done = f32[256,1024]{1,0:T(8,128)} async-done(((f32[32,1024]{1,0:T(8,128)}), f32[256,1024]{1,0:T(8,128)}) %all-gather.9.cloned.1.call-update) | async-done | bytes 1048592 | tf_op jit(solution)/shard_map/all_gather | solution.py:151
  572.3 2.3 broadcast_multiply_fusion.1
  (30 shorter events, 0.2 us)
Async XLA Ops:
  7.2 40.6 %all-gather.7.cloned.1.call-start = ((), (), s32[]{:S(2)}) async-start(), calls=%async_computation.7 | async-start | bytes 2621440 | tf_op jit(solution)/shard_map/all_gather | solution.py:88
  7.9 76.9 %all-gather.5.cloned.1.call-start = ((), (), s32[]{:S(2)}) async-start(), calls=%async_computation.6 | async-start | bytes 2621440 | tf_op jit(solution)/shard_map/all_gather | solution.py:92
  54.7 53.6 %all-to-all-start.1 = ((bf16[1024,8,128]{2,0,1:T(8,128)(2,1)}), bf16[1024,8,128]{2,0,1:T(8,128)(2,1)S(1)}, u32[]{:S(2)}, u32[]{:S(2)}) async-start(bf16[1024,8,128]{2,0,1:T(8,128)(2,1)} %copy.26), calls=%async_computation.1 | async-start | bytes 4194304 | tf_op jit(solution)/shard_map/all_to_all | solution.py:97
  108.4 4.7 copy-start.10
  108.4 8.4 %copy-start.9 = (bf16[2,128,128]{2,1,0:T(8,128)(2,1)S(1)}, bf16[2,128,128]{2,1,0:T(8,128)(2,1)}, u32[]{:S(2)}) copy-start(bf16[2,128,128]{2,1,0:T(8,128)(2,1)} %param.10) | copy-start | bytes 196612
  108.4 53.5 %all-to-all-start = ((bf16[1024,8,128]{0,2,1:T(8,128)(2,1)}), bf16[1024,8,128]{0,2,1:T(8,128)(2,1)}, u32[]{:S(2)}, u32[]{:S(2)}) async-start(bf16[1024,8,128]{0,2,1:T(8,128)(2,1)} %bitcast.90), calls=%async_computation | async-start | bytes 4194304 | tf_op jit(solution)/shard_map/all_to_all | solution.py:98
  161.9 2.2 copy-start
  161.9 2.9 copy-start.1
  173.4 1.4 copy-start.4
  173.4 2.0 copy-start.2
  182.3 53.4 %all-to-all-start.3 = ((bf16[8,1024,128]{1,2,0:T(8,128)(2,1)}), bf16[8,1024,128]{1,2,0:T(8,128)(2,1)}, u32[]{:S(2)}, u32[]{:S(2)}) async-start(bf16[8,1024,128]{1,2,0:T(8,128)(2,1)} %bitcast.84), calls=%async_computation.3 | async-start | bytes 4194304 | tf_op jit(solution)/shard_map/all_to_all | solution.py:132
  186.7 199.7 %reduce-scatter.9.cloned.1.call-start = ((), (), s32[]{:S(2)}) async-start(), calls=%async_computation.11 | async-start | bytes 4325376 | tf_op jit(solution)/shard_map/reduce_scatter | solution.py:144
  235.7 2.2 copy-start.11
  242.3 2.5 copy-start.7
  242.3 2.5 copy-start.8
  244.8 1.2 copy-start.5
  249.8 60.8 %all-to-all-start.2 = ((bf16[8,1024,128]{1,2,0:T(8,128)(2,1)}), bf16[8,1024,128]{1,2,0:T(8,128)(2,1)}, u32[]{:S(2)}, u32[]{:S(2)}) async-start(bf16[8,1024,128]{1,2,0:T(8,128)(2,1)} %bitcast.85), calls=%async_computation.2 | async-start | bytes 4194304 | tf_op jit(solution)/shard_map/all_to_all | solution.py:133
  254.1 274.9 %reduce-scatter.7.cloned.1.call-start = ((), (), s32[]{:S(2)}) async-start(), calls=%async_computation.10 | async-start | bytes 4325376 | tf_op jit(solution)/shard_map/reduce_scatter | solution.py:147
  322.7 226.3 %all-gather.11.cloned.1.call-start = ((), (), s32[]{:S(2)}) async-start(), calls=%async_computation.9 | async-start | bytes 1179648 | tf_op jit(solution)/shard_map/all_gather | solution.py:152
  386.5 185.8 %all-gather.9.cloned.1.call-start = ((), (), s32[]{:S(2)}) async-start(), calls=%async_computation.8 | async-start | bytes 1179648 | tf_op jit(solution)/shard_map/all_gather | solution.py:151
  386.8 4.5 copy-start.3
  386.8 4.5 copy-start.6
  529.0 5.0 collective-permute-start
  534.1 5.0 collective-permute-start.1
Sparse Core Ops, SparseCore 0:
  9.8 37.8 all-gather.6
  49.6 35.1 all-gather.4
  242.4 143.9 reduce-scatter.8
  388.6 140.3 reduce-scatter.6
  530.4 18.4 all-gather.10
  550.4 21.8 all-gather.8
